TPU v7x, 1024 devices: a whole 4x8x16 slice. The times are simulated.
1024 devices in a mesh: tm: 256 (over y, z, core), col: 4 (over x).
Axes of the slice: x: 4, y: 8, z: 16, core: 2. Of those that a mesh axis runs over, the one named last changes fastest.
Arguments:
- design: bfloat16 [32768, 2, 1024], P('tm', None, 'col'), may hold values from -512 to 512
- filter_taps: bfloat16 [256, 2, 512], replicated, may hold values from -3 to 3
- segment: int32 [32768], P('tm'), may hold values from 0 to 255, never falling along the last dimension, each value on 1 to 256 neighbouring positions
- valid_flags: int32 [32768], P('tm'), may hold values 0 or 1
- weights: float32 [2, 32768], P(None, 'tm'), may hold values from 0.05 to 20
- block_ids: int32 [4], replicated, may hold values from 0 to 3, each once
Outputs:
- normals: float32 [1024, 1024], P('tm', 'col')
All inputs are finite; a program needn't handle non-finite values. No bound on the sum of `valid_flags` on one device may be relied on, other than what follows from the above.
Results may differ from a plain program's by a relative error of at most 0.0013.
Values may be sent and summed in bfloat16 or wider, within the bound.
A program may use at most 32 MiB of HBM per device.

v0:
```python
import jax
import jax.numpy as jnp
from jax import lax
from jax.sharding import PartitionSpec as P


def from_behind(x, axis, by):
    devices = lax.axis_size(axis)
    pairs = [(i, i + by) for i in range(devices) if 0 <= i + by < devices]
    return lax.ppermute(x, axis, pairs)


def body(design, filter_taps, segment, valid_flags, weights, block_ids):
    row_count = design.shape[0]
    block_width = design.shape[2]
    tap_count = filter_taps.shape[2]
    seg_count = filter_taps.shape[0]
    block_count = block_ids.shape[0]
    halo_depth = (tap_count - 2) // row_count + 1
    window_rows = (halo_depth + 1) * row_count
    selector = (segment[:, None] == jnp.arange(seg_count, dtype=jnp.int32)[None, :]).astype(
        jnp.bfloat16
    )
    tap_rows = jnp.einsum(
        "ts,skj->ktj", selector, filter_taps, preferred_element_type=jnp.float32
    ).astype(jnp.bfloat16)
    reversed_taps = tap_rows[:, :, ::-1]
    offset = window_rows - row_count - tap_count + 1
    padded = jnp.pad(
        reversed_taps, ((0, 0), (0, 0), (offset, window_rows + 1 - offset - tap_count))
    )
    toeplitz = padded.reshape(2, row_count * (window_rows + 1))[
        :, : row_count * window_rows
    ].reshape(2, row_count, window_rows)
    pieces = []
    for hop_index in range(halo_depth):
        pieces.append(from_behind(design, "tm", halo_depth - hop_index))
    earlier = jnp.concatenate(pieces, axis=0)
    stacked = jnp.concatenate([earlier, design], axis=0)
    filtered = jnp.einsum(
        "kts,skc->tkc", toeplitz, stacked, preferred_element_type=jnp.float32
    ).astype(jnp.bfloat16)
    row_weight = (weights * valid_flags[None, :].astype(jnp.float32)).T
    owner = block_ids[:, None] == jnp.arange(block_count, dtype=jnp.int32)[None, :]
    column = lax.axis_index("col")
    gathered = lax.all_gather(filtered, "col", axis=2, tiled=True)
    ordered = (
        jnp.einsum(
            "tkdc,dp->tkpc",
            gathered.reshape(row_count, 2, block_count, block_width),
            owner.astype(jnp.bfloat16),
            preferred_element_type=jnp.float32,
        )
        .astype(jnp.bfloat16)
        .reshape(row_count, 2, block_count * block_width)
    )
    own_cols = lax.dynamic_slice_in_dim(ordered, column * block_width, block_width, 2)
    scaled = (own_cols.astype(jnp.float32) * row_weight[:, :, None]).astype(jnp.bfloat16)
    summed = lax.psum_scatter(
        jnp.einsum("tkp,tkq->pq", ordered, scaled, preferred_element_type=jnp.float32),
        "tm",
        scatter_dimension=0,
        tiled=True,
    )
    return summed / (2.0 * row_count * lax.axis_size("tm"))


def solution(mesh):
    return jax.shard_map(
        body,
        mesh=mesh,
        in_specs=(P("tm", None, "col"), P(), P("tm"), P("tm"), P(None, "tm"), P()),
        out_specs=P("tm", "col"),
        check_vma=False,
    )
```

profile of v0, /device:TPU:1, one launch (start us, length us, event | category | flops | bytes accessed | tf_op | source)
XLA Modules:
  0.0 415.5 jit_solution(5063828935992300153)
XLA Ops:
  6.5 0.0 copy-start
  6.5 0.0 copy-start.5
  6.5 0.0 all-reduce.4.cloned.1.call-start
  6.5 1.1 copy.25
  7.7 0.0 copy-start.4
  7.7 6.6 %collective-permute-start = (bf16[128,2,256]{0,2,1:T(8,128)(2,1)S(1)}, bf16[128,2,256]{0,2,1:T(8,128)(2,1)S(1)}, u32[]{:S(2)}, u32[]{:S(2)}) collective-permute-start(bf16[128,2,256]{0,2,1:T(8,128)(2,1)S(1)} %copy.25), channel_id=1, source_target_pairs={{0,16},{4,20},{8,24},{12,28},{16,32},{20,36},{24,40},{28,44},{32,4... | collective-permute-start | bytes 393224 | tf_op jit(solution)/shard_map/ppermute | solution.py:10
  14.3 7.9 %collective-permute-start.1 = (bf16[128,2,256]{0,2,1:T(8,128)(2,1)S(1)}, bf16[128,2,256]{0,2,1:T(8,128)(2,1)S(1)}, u32[]{:S(2)}, u32[]{:S(2)}) collective-permute-start(bf16[128,2,256]{0,2,1:T(8,128)(2,1)S(1)} %copy.25), channel_id=1, source_target_pairs={{0,12},{4,16},{8,20},{12,24},{16,28},{20,32},{24,36},{28,40},{32,4... | collective-permute-start | bytes 393224 | tf_op jit(solution)/shard_map/ppermute | solution.py:10
  22.2 4.0 collective-permute-start.2
  26.2 1.9 collective-permute-start.3
  28.1 0.0 copy-done.5
  28.1 0.0 copy-done
  28.1 0.0 copy-done.4
  28.1 0.0 copy-start.2
  28.2 0.3 fusion.1
  28.4 0.4 copy-done.2
  28.8 0.8 rev.3
  29.7 0.2 pad.4
  29.8 1.1 reshape.17
  30.9 0.0 copy-start.1
  30.9 0.7 copy-done.1
  31.6 0.0 collective-permute-done
  31.7 0.0 collective-permute-done.1
  31.7 0.0 collective-permute-done.2
  31.8 0.0 slice-start
  31.8 0.1 collective-permute-done.3
  31.9 0.8 slice-done
  32.7 0.3 fusion.2
  33.1 11.3 %all_gather.3 = bf16[128,2,1024]{0,2,1:T(8,128)(2,1)S(1)} all-gather(bf16[128,2,256]{0,2,1:T(8,128)(2,1)S(1)} %fusion.2), channel_id=1, replica_groups=mesh['tm'=256,'col'=4] {'col'}, dimensions={2}, use_global_device_ids=true | all-gather | bytes 655360 | tf_op jit(solution)/shard_map/all_gather | solution.py:46
  44.4 0.0 copy-start.3
  44.4 0.4 copy.31
  44.8 0.2 copy-done.3
  45.0 0.4 fusion
  45.5 0.2 reshape.20
  45.7 0.1 constant_dynamic-slice_fusion
  45.8 1.4 convolution_bitcast_fusion
  47.2 0.0 all-reduce.4.cloned.1.call-update
  47.2 1.3 dynamic-slice
  49.1 358.3 %all-reduce.4.cloned.1.call-done = f32[1024,256]{1,0:T(8,128)} async-done(((f32[1024,256]{1,0:T(8,128)}), f32[1024,256]{1,0:T(8,128)}) %all-reduce.4.cloned.1.call-update) | async-done | bytes 1048592
  407.4 1.3 dynamic-slice_multiply_fusion
  (7 shorter events, 0.2 us)
Async XLA Ops:
  6.5 21.6 %copy-start = (bf16[256,2,512]{2,1,0:T(2,128)(2,1)S(1)}, bf16[256,2,512]{2,1,0:T(2,128)(2,1)}, u32[]{:S(2)}) copy-start(bf16[256,2,512]{2,1,0:T(2,128)(2,1)} %param.7) | copy-start | bytes 1572868
  6.5 21.6 %copy-start.5 = (s32[128]{0:T(128)S(1)}, s32[128]{0:T(128)}, u32[]{:S(2)}) copy-start(s32[128]{0:T(128)} %param.9) | copy-start | bytes 1540
  6.5 400.9 %all-reduce.4.cloned.1.call-start = ((), (), s32[]{:S(2)}) async-start(), calls=%async_computation | async-start | bytes 2097152
  7.7 20.5 %copy-start.4 = (s32[128]{0:T(128)S(1)}, s32[128]{0:T(128)}, u32[]{:S(2)}) copy-start(s32[128]{0:T(128)} %param.8) | copy-start | bytes 1540
  7.7 24.0 %collective-permute-start = (bf16[128,2,256]{0,2,1:T(8,128)(2,1)S(1)}, bf16[128,2,256]{0,2,1:T(8,128)(2,1)S(1)}, u32[]{:S(2)}, u32[]{:S(2)}) collective-permute-start(bf16[128,2,256]{0,2,1:T(8,128)(2,1)S(1)} %copy.25), channel_id=1, source_target_pairs={{0,16},{4,20},{8,24},{12,28},{16,32},{20,36},{24,40},{28,44},{32,4... | collective-permute-start | bytes 393224 | tf_op jit(solution)/shard_map/ppermute | solution.py:10
  14.3 17.4 %collective-permute-start.1 = (bf16[128,2,256]{0,2,1:T(8,128)(2,1)S(1)}, bf16[128,2,256]{0,2,1:T(8,128)(2,1)S(1)}, u32[]{:S(2)}, u32[]{:S(2)}) collective-permute-start(bf16[128,2,256]{0,2,1:T(8,128)(2,1)S(1)} %copy.25), channel_id=1, source_target_pairs={{0,12},{4,16},{8,20},{12,24},{16,28},{20,32},{24,36},{28,40},{32,4... | collective-permute-start | bytes 393224 | tf_op jit(solution)/shard_map/ppermute | solution.py:10
  22.2 9.5 %collective-permute-start.2 = (bf16[128,2,256]{0,2,1:T(8,128)(2,1)S(1)}, bf16[128,2,256]{0,2,1:T(8,128)(2,1)S(1)}, u32[]{:S(2)}, u32[]{:S(2)}) collective-permute-start(bf16[128,2,256]{0,2,1:T(8,128)(2,1)S(1)} %copy.25), channel_id=1, source_target_pairs={{0,8},{4,12},{8,16},{12,20},{16,24},{20,28},{24,32},{28,36},{32,40... | collective-permute-start | bytes 393224 | tf_op jit(solution)/shard_map/ppermute | solution.py:10
  26.2 5.7 %collective-permute-start.3 = (bf16[128,2,256]{0,2,1:T(8,128)(2,1)S(1)}, bf16[128,2,256]{0,2,1:T(8,128)(2,1)S(1)}, u32[]{:S(2)}, u32[]{:S(2)}) collective-permute-start(bf16[128,2,256]{0,2,1:T(8,128)(2,1)S(1)} %copy.25), channel_id=1, source_target_pairs={{0,4},{4,8},{8,12},{12,16},{16,20},{20,24},{24,28},{28,32},{32,36}... | collective-permute-start | bytes 393224 | tf_op jit(solution)/shard_map/ppermute | solution.py:10
  28.1 0.7 copy-start.2
  30.9 0.7 copy-start.1
  31.8 1.0 slice-start
  44.4 0.7 copy-start.3
Sparse Core Ops, SparseCore 0:
  47.3 360.0 all-reduce.3
where the time goes:
time: 416 us
  waiting for transfers between devices  358 us (86%)
  starting transfers between devices  20.4 us (5%)
  between operations  14.3 us (3%)
  blocking collectives  11.3 us (3%)
  local copies, waits for them, and re-layouts  7.5 us (2%)
    unnamed x2, waiting for transfers between devices  358 us
    ppermute x4, starting transfers between devices, from_behind(): return lax.ppermute(x, axis, pairs)  20.4 us
    all_gather x1, blocking collectives, body(): gathered = lax.all_gather(filtered, 'col', axis=2, tiled=True)  11.3 us
  transfers between devices with their start and end apart: 5, of which 2 were waited for; matrix products, arithmetic and copies ran while one was open for 1% of the time, Pallas kernels for 0%

commit v1 on v0

v1 whole, which is shorter than its diff:
```python
import functools

import jax
import jax.numpy as jnp
from jax import lax
from jax.experimental import pallas as pl
from jax.experimental.pallas import tpu as pltpu
from jax.sharding import PartitionSpec as P

MESH = pl.DeviceIdType.MESH
NY, NZ, NX = 8, 16, 4
CHIPS = NY * NZ
EP = 128
CB = 256
HALF = 128
TAPS = 512
BLOCKS = 4
PARTS = 2
F32 = jnp.float32
BF16 = jnp.bfloat16


def kernel(
    rows_ref,
    tap_ref,
    weight_ref,
    ids_ref,
    out_ref,
    window,
    taps_all,
    weights_all,
    toeplitz,
    gathered_0,
    gathered_1,
    scaled,
    gram,
    up_slots,
    down_slots,
    y_slots,
    total,
    own_send,
    own_recv,
    halo_send,
    halo_recv,
    far_send,
    far_recv,
    side_send,
    side_recv,
    col_send,
    col_recv,
    q_send,
    q_recv,
    up_send,
    up_recv,
    down_send,
    down_recv,
    y_send,
    y_recv,
):
    tm = lax.axis_index("tm")
    x = lax.axis_index("col")
    h = lax.rem(tm, 2)
    chip = tm // 2
    z = lax.rem(chip, NZ)
    y = chip // NZ
    other = 1 - h
    y_core = lax.rem(y, 2)

    def dev(chip_at, core, x_at=x):
        return {"tm": chip_at * 2 + core, "col": x_at}

    def remote(src, dst, send_sem, recv_sem, device):
        return pltpu.make_async_remote_copy(
            src_ref=src, dst_ref=dst, send_sem=send_sem, recv_sem=recv_sem, device_id=device, device_id_type=MESH
        )

    next_chip = lax.rem(chip + 1, CHIPS)
    prev_chip = lax.rem(chip + CHIPS - 1, CHIPS)
    x_up, x_down = lax.rem(x + 1, NX), lax.rem(x + NX - 1, NX)
    z_up = y * NZ + lax.rem(z + 1, NZ)
    z_down = y * NZ + lax.rem(z + NZ - 1, NZ)

    barrier = pltpu.get_barrier_semaphore()

    def greet(device):
        pl.semaphore_signal(barrier, inc=1, device_id=device, device_id_type=MESH)

    greet(dev(chip, other))
    greet(dev(prev_chip, 0))
    greet(dev(prev_chip, 1))
    greet(dev(chip, h, x_up))
    greet(dev(chip, h, x_down))
    greet(dev(z_up, h))
    greet(dev(z_down, h))
    on_diagonal = h == y_core
    for source in range(NY):

        @pl.when(jnp.logical_not(jnp.logical_and(source == y, on_diagonal)))
        def _():
            greet(dev(source * NZ + z, y_core))

    pl.semaphore_wait(barrier, 15 - on_diagonal.astype(jnp.int32))

    sends = []
    gathered = (gathered_0, gathered_1)

    def start(copy):
        copy.start()
        sends.append(copy)

    own_rows = pl.ds(pl.multiple_of(2 * TAPS // 2 + EP * h, EP), EP)
    near_rows = pl.ds(pl.multiple_of(TAPS // 2 + EP * h, EP), EP)
    my_cols = pl.ds(pl.multiple_of(HALF * h, HALF), HALF)
    other_cols = pl.ds(pl.multiple_of(HALF * other, HALF), HALF)

    for k in range(2):
        for core in range(2):
            start(
                remote(
                    rows_ref.at[k, :, pl.ds(HALF * core, HALF)],
                    window.at[k, near_rows, :],
                    halo_send.at[k, core],
                    halo_recv.at[k, h],
                    dev(next_chip, core),
                )
            )
    start(remote(tap_ref, taps_all.at[h], side_send.at[0], side_recv.at[0], dev(chip, other)))
    start(remote(weight_ref, weights_all.at[h], side_send.at[1], side_recv.at[1], dev(chip, other)))
    for k in range(2):
        start(
            remote(
                rows_ref.at[k, :, other_cols],
                window.at[k, own_rows, :],
                own_send.at[k],
                own_recv.at[k],
                dev(chip, other),
            )
        )
    for k in range(2):
        window[k, own_rows, :] = rows_ref[k, :, my_cols]
    taps_all[h] = tap_ref[...]
    weights_all[h] = weight_ref[...]

    def arrived(dst, recv_sem):
        remote(dst, dst, own_send.at[0], recv_sem, dev(chip, other)).wait_recv()

    row_at = lax.broadcasted_iota(jnp.int32, (TAPS, TAPS), 0)
    col_at = lax.broadcasted_iota(jnp.int32, (TAPS, TAPS), 1)
    flip = (row_at + col_at == TAPS - 1).astype(F32).astype(BF16)
    first_row = jnp.where(chip == 0, TAPS, jnp.where(chip == 1, TAPS // 2, 0))
    lane = lax.broadcasted_iota(jnp.int32, (2 * EP, TAPS + 2 * EP), 1)

    def build(k):
        tap_rows = jnp.concatenate([taps_all[0, k], taps_all[1, k]], axis=0)
        flipped = jnp.dot(tap_rows, flip, preferred_element_type=F32)
        wide = jnp.concatenate([flipped, jnp.zeros((2 * EP, 2 * EP), F32)], axis=1)
        skewed = pltpu.roll(wide, 1, 1, stride=1, stride_axis=0)
        toeplitz[k] = jnp.where(lane >= first_row, skewed, 0.0).astype(BF16)

    other_tap = taps_all.at[other]
    arrived(other_tap, side_recv.at[0])
    arrived(weights_all.at[other], side_recv.at[1])
    build(0)
    for k in range(2):
        for core in range(2):
            arrived(window.at[k, pl.ds(TAPS // 2 + EP * core, EP), :], halo_recv.at[k, core])
        start(
            remote(
                window.at[k, pl.ds(TAPS // 2, TAPS // 2), :],
                window.at[k, pl.ds(0, TAPS // 2), :],
                far_send.at[k],
                far_recv.at[k],
                dev(next_chip, h),
            )
        )
        if k == 0:
            build(1)

    def slot(k, at):
        return gathered[k].at[at]

    def filter_and_send(k):
        arrived(window.at[k, pl.ds(pl.multiple_of(TAPS + EP * other, EP), EP), :], own_recv.at[k])
        near = jnp.dot(
            toeplitz[k, :, TAPS // 2 :], window[k, TAPS // 2 :, :], preferred_element_type=F32
        )
        arrived(window.at[k, pl.ds(0, TAPS // 2), :], far_recv.at[k])
        far = jnp.dot(
            toeplitz[k, :, : TAPS // 2], window[k, : TAPS // 2, :], preferred_element_type=F32
        )
        gathered[k][x] = (near + far).T.astype(BF16)
        start(remote(slot(k, x), slot(k, x), col_send.at[k, 0], col_recv.at[k, 0], dev(chip, h, x_up)))
        start(remote(slot(k, x), slot(k, x), col_send.at[k, 1], col_recv.at[k, 1], dev(chip, h, x_down)))

    def relay(k):
        if k == 0:
            arrived(slot(k, x_down), col_recv.at[k, 0])
            start(remote(slot(k, x_down), slot(k, x_down), col_send.at[k, 2], col_recv.at[k, 2], dev(chip, h, x_up)))
            arrived(slot(k, x_up), col_recv.at[k, 1])
        else:
            arrived(slot(k, x_up), col_recv.at[k, 1])
            start(remote(slot(k, x_up), slot(k, x_up), col_send.at[k, 2], col_recv.at[k, 2], dev(chip, h, x_down)))
            arrived(slot(k, x_down), col_recv.at[k, 0])

    def block_of(wanted):
        found = jnp.int32(0)
        for d in range(1, BLOCKS):
            found = jnp.where(ids_ref[d] == wanted, d, found)
        return found

    def scale(k):
        arrived(slot(k, lax.rem(x + 2, NX)), col_recv.at[k, 2])
        row_weight = jnp.concatenate([weights_all[0, k : k + 1], weights_all[1, k : k + 1]], axis=1)
        mine = gathered[k][block_of(x)].astype(F32) * row_weight
        scaled[k, h] = mine.astype(BF16)
        start(remote(scaled.at[k, h], scaled.at[k, h], q_send.at[k], q_recv.at[k], dev(chip, other)))

    def multiply(k):
        arrived(scaled.at[k, other], q_recv.at[k])
        right = scaled[k].reshape(CB, 2 * EP)
        for b in range(BLOCKS):
            left = gathered[k][block_of(b)]
            product = lax.dot_general(
                left, right, (((1,), (1,)), ((), ())), preferred_element_type=F32
            ).reshape(NZ, 8, CB)
            if k == 0:
                gram[:, b] = product
            else:
                gram[:, b] += product

    filter_and_send(0)
    relay(0)
    filter_and_send(1)
    scale(0)
    relay(1)
    multiply(0)
    scale(1)
    multiply(1)

    size = BLOCKS // PARTS
    for step in range(1, NZ // 2 + 1):
        for part in range(PARTS):
            piece = pl.ds(part * size, size)
            for way in range(2):
                slots, send_sem, recv_sem = (
                    (up_slots, up_send, up_recv) if way == 0 else (down_slots, down_send, down_recv)
                )
                if way == 1 and step == NZ // 2:
                    continue
                if way == 0:
                    dest = lax.rem(z + NZ // 2 + 1 - step, NZ)
                else:
                    dest = lax.rem(z + NZ // 2 + step, NZ)
                if step == 1:
                    src = gram.at[dest, piece]
                else:
                    src = slots.at[step - 2, piece]
                    arrived(src, recv_sem.at[step - 2, part])
                    slots[step - 2, piece] += gram[dest, piece]
                start(
                    remote(
                        src,
                        slots.at[step - 1, piece],
                        send_sem.at[step - 1, part],
                        recv_sem.at[step - 1, part],
                        dev(z_up if way == 0 else z_down, h),
                    )
                )
    for part in range(PARTS):
        piece = pl.ds(part * size, size)
        arrived(up_slots.at[NZ // 2 - 1, piece], up_recv.at[NZ // 2 - 1, part])
        arrived(down_slots.at[NZ // 2 - 2, piece], down_recv.at[NZ // 2 - 2, part])
        total[piece] = gram[z, piece] + up_slots[NZ // 2 - 1, piece] + down_slots[NZ // 2 - 2, piece]

    for b in range(BLOCKS):
        for core in range(2):
            remote_one = jnp.logical_not(
                jnp.logical_and(jnp.logical_and(2 * b + h == y, on_diagonal), h == core)
            )
            copy = remote(
                total.at[b],
                y_slots.at[y],
                y_send.at[b, core],
                y_recv.at[y],
                dev((2 * b + h) * NZ + z, core),
            )

            @pl.when(remote_one)
            def _():
                copy.start()

    @pl.when(on_diagonal)
    def _():
        y_slots[y] = total[y // 2]

    for source in range(NY):

        @pl.when(jnp.logical_not(jnp.logical_and(source == y, on_diagonal)))
        def _():
            arrived(y_slots.at[source], y_recv.at[source])

    result = y_slots[0]
    for source in range(1, NY):
        result = result + y_slots[source]
    out_ref[...] = jnp.where(h == 0, result[:4], result[4:]) * (1.0 / 65536.0)

    for copy in sends:
        copy.wait_send()
    for b in range(BLOCKS):
        for core in range(2):
            remote_one = jnp.logical_not(
                jnp.logical_and(jnp.logical_and(2 * b + h == y, on_diagonal), h == core)
            )

            @pl.when(remote_one)
            def _():
                remote(
                    total.at[b],
                    y_slots.at[y],
                    y_send.at[b, core],
                    y_recv.at[y],
                    dev((2 * b + h) * NZ + z, core),
                ).wait_send()


def body(design, filter_taps, segment, valid_flags, weights, block_ids):
    seg_count = filter_taps.shape[0]
    selector = (segment[:, None] == jnp.arange(seg_count, dtype=jnp.int32)[None, :]).astype(BF16)
    tap_rows = jnp.einsum("ts,skj->ktj", selector, filter_taps, preferred_element_type=F32).astype(BF16)
    rows = jnp.transpose(design, (1, 0, 2))
    row_weight = weights * valid_flags[None, :].astype(F32)
    vmem = pl.BlockSpec(memory_space=pltpu.VMEM)
    dma = pltpu.SemaphoreType.DMA
    steps = NZ // 2
    return pl.pallas_call(
        kernel,
        out_shape=jax.ShapeDtypeStruct((4, CB), F32),
        in_specs=[vmem, vmem, vmem, pl.BlockSpec(memory_space=pltpu.SMEM)],
        out_specs=vmem,
        scratch_shapes=[
            pltpu.VMEM((2, TAPS + 2 * EP, HALF), BF16),
            pltpu.VMEM((2, 2, EP, TAPS), BF16),
            pltpu.VMEM((2, 2, EP), F32),
            pltpu.VMEM((2, 2 * EP, TAPS + 2 * EP), BF16),
            pltpu.VMEM((NX, HALF, 2 * EP), BF16),
            pltpu.VMEM((NX, HALF, 2 * EP), BF16),
            pltpu.VMEM((2, 2, HALF, 2 * EP), BF16),
            pltpu.VMEM((NZ, BLOCKS, 8, CB), F32),
            pltpu.VMEM((steps, BLOCKS, 8, CB), F32),
            pltpu.VMEM((steps - 1, BLOCKS, 8, CB), F32),
            pltpu.VMEM((NY, 8, CB), F32),
            pltpu.VMEM((BLOCKS, 8, CB), F32),
            dma((2,)),
            dma((2,)),
            dma((2, 2)),
            dma((2, 2)),
            dma((2,)),
            dma((2,)),
            dma((2,)),
            dma((2,)),
            dma((2, 3)),
            dma((2, 3)),
            dma((2,)),
            dma((2,)),
            dma((steps, PARTS)),
            dma((steps, PARTS)),
            dma((steps - 1, PARTS)),
            dma((steps - 1, PARTS)),
            dma((BLOCKS, 2)),
            dma((NY,)),
        ],
        compiler_params=pltpu.CompilerParams(collective_id=0, has_side_effects=True),
    )(rows, tap_rows, row_weight, block_ids)


def solution(mesh):
    return jax.shard_map(
        body,
        mesh=mesh,
        in_specs=(P("tm", None, "col"), P(), P("tm"), P("tm"), P(None, "tm"), P()),
        out_specs=P("tm", "col"),
        check_vma=False,
    )
```

time: 416 us -> 78.6 us (0.19)
  waiting for transfers between devices: 358 us -> 0 us
  Pallas kernels: 0 us -> 72.6 us
  starting transfers between devices: 20.4 us -> 0 us
  between operations: 14.3 us -> 0.01 us
  blocking collectives: 11.3 us -> 0 us
    unnamed x2 -> x0, waiting for transfers between devices: 358 us -> none
    pallas_call x0 -> x1, Pallas kernels: none -> 72.6 us  [body(): pl.pallas_call(kernel, out_shape=jax.ShapeDtypeStruct((4, CB), F32), in_s...]
    ppermute x4 -> x0, starting transfers between devices: 20.4 us -> none  [from_behind(): return lax.ppermute(x, axis, pairs)]
    all_gather x1 -> x0, blocking collectives: 11.3 us -> none  [body(): gathered = lax.all_gather(filtered, 'col', axis=2, tiled=True)]
  transfers between devices with their start and end apart: 5 -> 0, of which waited for: 2 -> 0; matrix products, arithmetic and copies ran while one was open for 1% -> 0% of each run, Pallas kernels for 0% -> 0%
where the time goes in v1:
time: 78.6 us; the launch traced here: 78.4 us
  Pallas kernels  72.6 us (92%)
  local copies, waits for them, and re-layouts  3.53 us (4%)
  other arithmetic  1.29 us (2%)
  matrix products  0.96 us (1%)
    pallas_call x1, Pallas kernels, body(): pl.pallas_call(kernel, out_shape=jax.ShapeDtypeStruct((4, CB), F32), in_s...  72.6 us
    unnamed x8, local copies, waits for them, and re-layouts  3.53 us

profile of v1, /device:TPU:1, one launch (start us, length us, event | category | flops | bytes accessed | tf_op | source)
XLA Modules:
  0.0 78.4 jit_solution(6750042314453447427)
XLA Ops:
  0.0 0.0 copy-start
  0.0 0.0 copy-start.1
  0.0 0.7 convert_element_type.12
  0.7 0.0 copy-done.1
  0.7 0.6 broadcast_multiply_fusion.weight_ref
  1.3 1.6 %copy.12 = bf16[128,2,256]{2,0,1:T(8,128)(2,1)} copy(bf16[128,2,256]{2,1,0:T(2,128)(2,1)} %param.6) | data formatting | bytes 262144 | tf_op args[0]
  2.9 0.0 copy-start.2
  2.9 0.0 copy-done
  2.9 0.7 copy-done.2
  3.6 1.0 %fusion.tap_ref = bf16[2,128,512]{2,1,0:T(8,128)(2,1)} fusion(bf16[256,2,512]{2,1,0:T(2,128)(2,1)S(1)} %copy-done, s32[128]{0:T(128)S(1)} %copy-done.2), kind=kOutput, calls=%fused_computation.1 | convolution fusion | flops 67272704 | bytes 786944 | tf_op jit(solution)/shard_map/ts,skj->ktj/dot_general | solution.py:329
  4.5 72.6 %shard_map.64 = f32[4,256]{1,0:T(4,128)} custom-call(bf16[2,128,256]{2,1,0:T(8,128)(2,1)} %bitcast.8, bf16[2,128,512]{2,1,0:T(8,128)(2,1)} %fusion.tap_ref, f32[2,128]{1,0:T(2,128)} %broadcast_multiply_fusion.weight_ref, s32[4]{0:T(128)} %ids_ref.1), custom_call_target="tpu_custom_call" | custom-call | tf_op jit(solution)/shard_map/pallas_call | solution.py:335
  77.1 1.3 %copy.14 = f32[4,256]{1,0:T(4,128)} copy(f32[4,256]{1,0:T(4,128)} %shard_map.64) | data formatting | bytes 8192
Async XLA Ops:
  0.0 2.9 %copy-start = (bf16[256,2,512]{2,1,0:T(2,128)(2,1)S(1)}, bf16[256,2,512]{2,1,0:T(2,128)(2,1)}, u32[]{:S(2)}) copy-start(bf16[256,2,512]{2,1,0:T(2,128)(2,1)} %param.7) | copy-start | bytes 1572868
  0.0 0.7 copy-start.1
  2.9 0.7 copy-start.2

commit v2 on v1

v2 whole, which is shorter than its diff:
```python
import jax
import jax.numpy as jnp
from jax import lax
from jax.experimental import pallas as pl
from jax.experimental.pallas import tpu as pltpu
from jax.sharding import PartitionSpec as P

MESH = pl.DeviceIdType.MESH
NY, NZ, NX = 8, 16, 4
CHIPS = NY * NZ
EP = 128
CB = 256
HALF = 128
TAPS = 512
SEGS = 256
BLOCKS = 4
SPAN = 2 * EP
WINDOW = TAPS + SPAN
F32 = jnp.float32
BF16 = jnp.bfloat16

COLLECTOR = {8: 5, 7: 5, -7: -5, 6: 5, -6: -5, 4: 5, -4: -5, 3: 5, -3: -5, 2: 0, -2: 0, 1: 0, -1: 0}
SOURCES = list(COLLECTOR)


def kernel(
    design_ref,
    taps_ref,
    segment_ref,
    valid_ref,
    weight_ref,
    ids_ref,
    out_ref,
    rows,
    window,
    side_weight,
    side_segment,
    toeplitz,
    gathered_0,
    gathered_1,
    scaled,
    gram_z,
    gram_y,
    z_slots,
    middle,
    z_tops,
    total_z,
    z_final,
    y_slots,
    total_y,
    y_final,
    near_send,
    near_recv,
    far_send,
    far_recv,
    own_send,
    own_recv,
    side_send,
    side_recv,
    col_send,
    col_recv,
    q_send,
    q_recv,
    z_send,
    z_recv,
    top_send,
    top_recv,
    zf_send,
    zf_recv,
    y_send,
    y_recv,
    yf_send,
    yf_recv,
    token,
):
    tm = lax.axis_index("tm")
    x = lax.axis_index("col")
    h = lax.rem(tm, 2)
    chip = tm // 2
    z = lax.rem(chip, NZ)
    y = chip // NZ
    other = 1 - h
    y_core = lax.rem(y, 2)
    keeps = h == y_core
    gathered = (gathered_0, gathered_1)

    def dev(chip_at, core, x_at=x):
        return {"tm": chip_at * 2 + core, "col": x_at}

    def along_z(offset, core=h):
        return dev(y * NZ + lax.rem(z + offset + NZ, NZ), core)

    def along_y(offset, core=h):
        return dev(lax.rem(y + offset + NY, NY) * NZ + z, core)

    def remote(src, dst, send_sem, recv_sem, device):
        return pltpu.make_async_remote_copy(
            src_ref=src, dst_ref=dst, send_sem=send_sem, recv_sem=recv_sem, device_id=device, device_id_type=MESH
        )

    pair = dev(chip, other)
    next_chip = lax.rem(chip + 1, CHIPS)
    prev_chip = lax.rem(chip + CHIPS - 1, CHIPS)
    x_up, x_down = lax.rem(x + 1, NX), lax.rem(x + NX - 1, NX)
    x_far = lax.rem(x + 2, NX)

    sends = []

    def start(copy):
        copy.start()
        sends.append(copy)

    def arrived(dst, recv_sem):
        remote(dst, dst, own_send.at[0], recv_sem, pair).wait_recv()

    def tell(which, devices):
        for device in devices:
            pl.semaphore_signal(token.at[which], inc=1, device_id=device, device_id_type=MESH)

    barrier = pltpu.get_barrier_semaphore()
    greeted = [
        pair,
        dev(prev_chip, 0),
        dev(prev_chip, 1),
        dev(chip, h, x_up),
        dev(chip, h, x_down),
        along_z(1),
        along_z(-1),
        along_y(1),
        along_y(-1),
    ]
    for device in greeted:
        pl.semaphore_signal(barrier, inc=1, device_id=device, device_id_type=MESH)
    for k in range(2):
        rows[k] = design_ref[:, k, :]
    pl.semaphore_wait(barrier, len(greeted))

    own_rows = pl.ds(pl.multiple_of(TAPS + EP * h, EP), EP)
    near_rows = pl.ds(pl.multiple_of(TAPS // 2 + EP * h, EP), EP)
    my_cols = pl.ds(pl.multiple_of(HALF * h, HALF), HALF)
    other_cols = pl.ds(pl.multiple_of(HALF * other, HALF), HALF)

    for k in range(2):
        for core in range(2):
            start(
                remote(
                    rows.at[k, :, pl.ds(HALF * core, HALF)],
                    window.at[k, near_rows, :],
                    near_send.at[k, core],
                    near_recv.at[k, h],
                    dev(next_chip, core),
                )
            )
    side_weight[h] = weight_ref[...] * valid_ref[...].astype(F32)
    start(remote(segment_ref, side_segment.at[h], side_send.at[0], side_recv.at[0], pair))
    for k in range(2):
        start(
            remote(
                rows.at[k, :, other_cols], window.at[k, own_rows, :], own_send.at[k], own_recv.at[k], pair
            )
        )
    tell(0, [along_z(1), along_z(-1)])
    tell(1, [along_y(1), along_y(-1)])
    for k in range(2):
        window[k, own_rows, :] = rows[k, :, my_cols]
    side_segment[h] = segment_ref[...]
    start(remote(side_weight.at[h], side_weight.at[h], side_send.at[1], side_recv.at[1], pair))

    flip = (
        lax.broadcasted_iota(jnp.int32, (TAPS, TAPS), 0) + lax.broadcasted_iota(jnp.int32, (TAPS, TAPS), 1)
        == TAPS - 1
    ).astype(F32).astype(BF16)
    first_row = jnp.where(chip == 0, TAPS, jnp.where(chip == 1, TAPS // 2, 0))
    lane = lax.broadcasted_iota(jnp.int32, (SPAN, WINDOW), 1)
    arrived(side_segment.at[other], side_recv.at[0])
    segments = jnp.concatenate([side_segment[0], side_segment[1]], axis=1)
    selector = (lax.broadcasted_iota(jnp.int32, (SEGS, SPAN), 0) == segments).astype(F32).astype(BF16)

    def build(k):
        tap_rows = lax.dot_general(
            selector, taps_ref[:, k, :], (((0,), (0,)), ((), ())), preferred_element_type=F32
        ).astype(BF16)
        flipped = jnp.dot(tap_rows, flip, preferred_element_type=F32)
        wide = jnp.concatenate([flipped, jnp.zeros((SPAN, SPAN), F32)], axis=1)
        skewed = pltpu.roll(wide, 1, 1, stride=1, stride_axis=0)
        toeplitz[k] = jnp.where(lane >= first_row, skewed, 0.0).astype(BF16)

    def pass_on(k):
        for core in range(2):
            arrived(window.at[k, pl.ds(TAPS // 2 + EP * core, EP), :], near_recv.at[k, core])
        start(
            remote(
                window.at[k, pl.ds(TAPS // 2, TAPS // 2), :],
                window.at[k, pl.ds(0, TAPS // 2), :],
                far_send.at[k],
                far_recv.at[k],
                dev(next_chip, h),
            )
        )

    build(0)
    pass_on(0)
    pl.semaphore_wait(token.at[0], 2)
    pl.semaphore_wait(token.at[1], 2)
    tell(2, [along_z(2), along_z(-2)])
    tell(3, [along_y(2), along_y(-2)])
    pass_on(1)
    build(1)
    pl.semaphore_wait(token.at[2], 2)
    pl.semaphore_wait(token.at[3], 2)
    tell(4, [along_z(4), along_z(-4)])

    def piece(k, at, part):
        return gathered[k].at[at, pl.ds(part * HALF // 2, HALF // 2)]

    def send_piece(k, at, part, which, x_to):
        start(remote(piece(k, at, part), piece(k, at, part), col_send.at[k, which], col_recv.at[k, which], dev(chip, h, x_to)))

    def filter_and_send(k):
        arrived(window.at[k, pl.ds(pl.multiple_of(TAPS + EP * other, EP), EP), :], own_recv.at[k])
        near = jnp.dot(toeplitz[k, :, TAPS // 2 :], window[k, TAPS // 2 :, :], preferred_element_type=F32)
        arrived(window.at[k, pl.ds(0, TAPS // 2), :], far_recv.at[k])
        far = jnp.dot(toeplitz[k, :, : TAPS // 2], window[k, : TAPS // 2, :], preferred_element_type=F32)
        gathered[k][x] = (near + far).T.astype(BF16)
        send_piece(k, x, 0, 0, x_up)
        send_piece(k, x, 1, 1, x_down)
        send_piece(k, x, 1, 2, x_up)
        send_piece(k, x, 0, 3, x_down)

    def relay(k):
        arrived(piece(k, x_down, 0), col_recv.at[k, 0])
        send_piece(k, x_down, 0, 4, x_up)
        arrived(piece(k, x_up, 1), col_recv.at[k, 1])
        send_piece(k, x_up, 1, 5, x_down)

    def block_of(wanted):
        found = jnp.int32(0)
        for d in range(1, BLOCKS):
            found = jnp.where(ids_ref[d] == wanted, d, found)
        return found

    def scale(k):
        arrived(piece(k, x_down, 1), col_recv.at[k, 2])
        arrived(piece(k, x_up, 0), col_recv.at[k, 3])
        arrived(piece(k, x_far, 0), col_recv.at[k, 4])
        arrived(piece(k, x_far, 1), col_recv.at[k, 5])
        row_weight = jnp.concatenate([side_weight[0, k : k + 1], side_weight[1, k : k + 1]], axis=1)
        scaled[k, h] = (gathered[k][block_of(x)].astype(F32) * row_weight).astype(BF16)
        start(remote(scaled.at[k, h], scaled.at[k, h], q_send.at[k], q_recv.at[k], pair))

    def y_copy(b):
        step = lax.rem(2 * b + h - y + NY, NY)
        return remote(gram_y.at[b], y_slots.at[step], y_send.at[b], y_recv.at[step], dev((2 * b + h) * NZ + z, h))

    def multiply(k):
        arrived(scaled.at[k, other], q_recv.at[k])
        right = scaled[k].reshape(CB, SPAN)
        for b in range(BLOCKS):
            product = lax.dot_general(
                gathered[k][block_of(b)], right, (((1,), (1,)), ((), ())), preferred_element_type=F32
            ).reshape(NZ, 8, CB)
            if k == 0:
                gram_z[:, b] = product[:, :, :HALF]
                gram_y[b] = product[:, :, HALF:]
            else:
                gram_z[:, b] += product[:, :, :HALF]
                gram_y[b] += product[:, :, HALF:]

    filter_and_send(0)
    pl.semaphore_wait(token.at[4], 2)
    tell(5, [pair])
    relay(0)
    filter_and_send(1)
    arrived(side_weight.at[other], side_recv.at[1])
    scale(0)
    relay(1)
    multiply(0)
    scale(1)
    pl.semaphore_wait(token.at[5], 1)
    multiply(1)

    for index, s in enumerate(SOURCES):
        if index == 4:
            for b in range(BLOCKS):

                @pl.when(2 * b + h != y)
                def _():
                    y_copy(b).start()

        start(
            remote(
                gram_z.at[lax.rem(z - s + NZ, NZ)],
                z_slots.at[index],
                z_send.at[index],
                z_recv.at[index],
                along_z(COLLECTOR[s] - s),
            )
        )

    def collect(into, own):
        added = gram_z[own]
        for index, s in enumerate(SOURCES):
            if COLLECTOR[s] == into:
                arrived(z_slots.at[index], z_recv.at[index])
                added = added + z_slots[index]
        return added

    for index, place in enumerate((-5, 5)):
        middle[index] = collect(place, lax.rem(z - place + NZ, NZ))
        start(
            remote(middle.at[index], z_tops.at[index], top_send.at[index], top_recv.at[index], along_z(-place))
        )

    def yf_copies():
        out = [remote(total_y.at[z], y_final.at[0], yf_send.at[0, 0], yf_recv.at[0], pair)]
        for step in range(1, NZ):
            for core in range(2):
                out.append(
                    remote(
                        total_y.at[lax.rem(z + step, NZ)],
                        y_final.at[step],
                        yf_send.at[step, core],
                        yf_recv.at[step],
                        along_z(step, core),
                    )
                )
        return out

    @pl.when(keeps)
    def _():
        added = gram_y[y // 2]
        for step in range(1, NY):
            arrived(y_slots.at[step], y_recv.at[step])
            added = added + y_slots[step]
        total_y[...] = added
        copies = yf_copies()
        for step in (8, 7, 9, 6, 10, 5, 11, 4, 12, 3, 13, 2, 14, 1, 15):
            copies[2 * step - 1].start()
            copies[2 * step].start()
        copies[0].start()
        y_final[0] = total_y[z]

    summed = collect(0, z)
    for index in range(2):
        arrived(z_tops.at[index], top_recv.at[index])
        summed = summed + z_tops[index]
    total_z[...] = summed

    def zf_copy(b, core):
        step = lax.rem(2 * b + h - y + NY, NY)
        return remote(
            total_z.at[b], z_final.at[step], zf_send.at[b, core], zf_recv.at[step], dev((2 * b + h) * NZ + z, core)
        )

    def for_each_zf(act):
        for b in range(BLOCKS):
            for core in range(2):

                @pl.when(jnp.logical_not(jnp.logical_and(2 * b + h == y, h == core)))
                def _():
                    act(zf_copy(b, core))

    for_each_zf(lambda copy: copy.start())

    @pl.when(keeps)
    def _():
        z_final[0] = total_z[y // 2]

    @pl.when(jnp.logical_not(keeps))
    def _():
        arrived(y_final.at[0], yf_recv.at[0])
        arrived(z_final.at[0], zf_recv.at[0])

    right = y_final[0]
    for step in range(1, NZ):
        arrived(y_final.at[step], yf_recv.at[step])
        right = right + y_final[step]
    left = z_final[0]
    for step in range(1, NY):
        arrived(z_final.at[step], zf_recv.at[step])
        left = left + z_final[step]
    result = jnp.concatenate([left, right], axis=1) * (1.0 / 65536.0)
    out_ref[...] = jnp.where(h == 0, result[:4], result[4:])

    for copy in sends:
        copy.wait_send()
    for b in range(BLOCKS):

        @pl.when(2 * b + h != y)
        def _():
            y_copy(b).wait_send()

    for_each_zf(lambda copy: copy.wait_send())

    @pl.when(keeps)
    def _():
        for copy in yf_copies():
            copy.wait_send()


def body(design, filter_taps, segment, valid_flags, weights, block_ids):
    vmem = pl.BlockSpec(memory_space=pltpu.VMEM)
    dma = pltpu.SemaphoreType.DMA
    kinds = len(SOURCES)
    return pl.pallas_call(
        kernel,
        out_shape=jax.ShapeDtypeStruct((4, CB), F32),
        in_specs=[vmem] * 5 + [pl.BlockSpec(memory_space=pltpu.SMEM)],
        out_specs=vmem,
        scratch_shapes=[
            pltpu.VMEM((2, EP, CB), BF16),
            pltpu.VMEM((2, WINDOW, HALF), BF16),
            pltpu.VMEM((2, 2, EP), F32),
            pltpu.VMEM((2, 1, EP), jnp.int32),
            pltpu.VMEM((2, SPAN, WINDOW), BF16),
            pltpu.VMEM((NX, HALF, SPAN), BF16),
            pltpu.VMEM((NX, HALF, SPAN), BF16),
            pltpu.VMEM((2, 2, HALF, SPAN), BF16),
            pltpu.VMEM((NZ, BLOCKS, 8, HALF), F32),
            pltpu.VMEM((BLOCKS, NZ, 8, HALF), F32),
            pltpu.VMEM((kinds, BLOCKS, 8, HALF), F32),
            pltpu.VMEM((2, BLOCKS, 8, HALF), F32),
            pltpu.VMEM((2, BLOCKS, 8, HALF), F32),
            pltpu.VMEM((BLOCKS, 8, HALF), F32),
            pltpu.VMEM((NY, 8, HALF), F32),
            pltpu.VMEM((NY, NZ, 8, HALF), F32),
            pltpu.VMEM((NZ, 8, HALF), F32),
            pltpu.VMEM((NZ, 8, HALF), F32),
            dma((2, 2)),
            dma((2, 2)),
            dma((2,)),
            dma((2,)),
            dma((2,)),
            dma((2,)),
            dma((2,)),
            dma((2,)),
            dma((2, 6)),
            dma((2, 6)),
            dma((2,)),
            dma((2,)),
            dma((kinds,)),
            dma((kinds,)),
            dma((2,)),
            dma((2,)),
            dma((BLOCKS, 2)),
            dma((NY,)),
            dma((BLOCKS,)),
            dma((NY,)),
            dma((NZ, 2)),
            dma((NZ,)),
            pltpu.SemaphoreType.REGULAR((6,)),
        ],
        compiler_params=pltpu.CompilerParams(collective_id=0, has_side_effects=True),
    )(design, filter_taps, segment.reshape(1, EP), valid_flags.reshape(1, EP), weights, block_ids)


def solution(mesh):
    return jax.shard_map(
        body,
        mesh=mesh,
        in_specs=(P("tm", None, "col"), P(), P("tm"), P("tm"), P(None, "tm"), P()),
        out_specs=P("tm", "col"),
        check_vma=False,
    )
```

time: 78.6 us -> 61.4 us (0.78)
  Pallas kernels: 72.6 us -> 59.9 us
  local copies, waits for them, and re-layouts: 3.53 us -> 1.28 us
  other arithmetic: 1.29 us -> 0 us
  matrix products: 0.96 us -> 0 us
    pallas_call x1, Pallas kernels: 72.6 us -> 59.9 us  [body(): pl.pallas_call(kernel, out_shape=jax.ShapeDtypeStruct((4, CB), F32), in_s...]
    unnamed x8 -> x1, local copies, waits for them, and re-layouts: 3.53 us -> 1.28 us
    dot_general x1 -> x0, matrix products: 0.96 us -> none  [body(): jnp.einsum('ts,skj->ktj', selector, filter_taps, preferred_element_type=F32)]
where the time goes in v2:
time: 61.4 us; the launch traced here: 61.2 us
  Pallas kernels  59.9 us (98%)
  local copies, waits for them, and re-layouts  1.28 us (2%)
    pallas_call x1, Pallas kernels, body(): pl.pallas_call(kernel, out_shape=jax.ShapeDtypeStruct((4, CB), F32), in_s...  59.9 us
    unnamed x1, local copies, waits for them, and re-layouts  1.28 us

profile of v2, /device:TPU:1, one launch (start us, length us, event | category | flops | bytes accessed | tf_op | source)
XLA Modules:
  0.0 61.2 jit_solution(12596240712685681423)
XLA Ops:
  0.0 59.9 %shard_map.64 = f32[4,256]{1,0:T(4,128)} custom-call(bf16[128,2,256]{2,1,0:T(2,128)(2,1)} %design_ref.1, bf16[256,2,512]{2,1,0:T(2,128)(2,1)} %taps_ref.1, s32[1,128]{1,0:T(1,128)} %bitcast.2, s32[1,128]{1,0:T(1,128)} %bitcast.3, f32[2,128]{1,0:T(2,128)} %weight_ref.1, s32[4]{0:T(128)} %ids_ref.1), custom_call_target="tpu_custom_call" | custom-call | tf_op jit(solution)/shard_map/pallas_call | solution.py:405
  59.9 1.3 %copy.8 = f32[4,256]{1,0:T(4,128)} copy(f32[4,256]{1,0:T(4,128)} %shard_map.64) | data formatting | bytes 8192

commit v3 on v2

--- a/solution.py
+++ b/solution.py
@@ -24,15 +24,22 @@
 
 
 def kernel(
+    design_in,
+    taps_in,
+    segment_in,
+    valid_in,
+    weight_in,
+    ids_in,
+    out_ref,
     design_ref,
     taps_ref,
     segment_ref,
     valid_ref,
     weight_ref,
     ids_ref,
-    out_ref,
     rows,
     window,
+    side_mine,
     side_weight,
     side_segment,
     toeplitz,
@@ -49,10 +56,10 @@
     y_slots,
     total_y,
     y_final,
-    near_send,
-    near_recv,
-    far_send,
-    far_recv,
+    first_send,
+    first_recv,
+    last_send,
+    last_recv,
     own_send,
     own_recv,
     side_send,
@@ -72,7 +79,24 @@
     yf_send,
     yf_recv,
     token,
+    load_sem,
 ):
+    loads = [
+        pltpu.make_async_copy(src, dst, load_sem.at[index])
+        for index, (src, dst) in enumerate(
+            (
+                (design_in, design_ref),
+                (segment_in, segment_ref),
+                (valid_in, valid_ref),
+                (weight_in, weight_ref),
+                (taps_in, taps_ref),
+                (ids_in, ids_ref),
+            )
+        )
+    ]
+    for load in loads:
+        load.start()
+
     tm = lax.axis_index("tm")
     x = lax.axis_index("col")
     h = lax.rem(tm, 2)
@@ -122,6 +146,8 @@
         pair,
         dev(prev_chip, 0),
         dev(prev_chip, 1),
+        dev(next_chip, 0),
+        dev(next_chip, 1),
         dev(chip, h, x_up),
         dev(chip, h, x_down),
         along_z(1),
@@ -131,48 +157,61 @@
     ]
     for device in greeted:
         pl.semaphore_signal(barrier, inc=1, device_id=device, device_id_type=MESH)
+    loads[0].wait()
     for k in range(2):
         rows[k] = design_ref[:, k, :]
     pl.semaphore_wait(barrier, len(greeted))
 
-    own_rows = pl.ds(pl.multiple_of(TAPS + EP * h, EP), EP)
-    near_rows = pl.ds(pl.multiple_of(TAPS // 2 + EP * h, EP), EP)
+    first_rows = pl.ds(pl.multiple_of(EP * h, EP), EP)
+    own_rows = pl.ds(pl.multiple_of(SPAN + EP * h, EP), EP)
+    last_rows = pl.ds(pl.multiple_of(2 * SPAN + EP * h, EP), EP)
     my_cols = pl.ds(pl.multiple_of(HALF * h, HALF), HALF)
     other_cols = pl.ds(pl.multiple_of(HALF * other, HALF), HALF)
 
+    for load in loads[1:4]:
+        load.wait()
+    side_mine[...] = weight_ref[...] * valid_ref[...].astype(F32)
+    for core in range(2):
+        start(
+            remote(
+                segment_ref, side_segment.at[h], side_send.at[0, core], side_recv.at[0, h], dev(prev_chip, core)
+            )
+        )
     for k in range(2):
         for core in range(2):
+            half = rows.at[k, :, pl.ds(HALF * core, HALF)]
             start(
                 remote(
-                    rows.at[k, :, pl.ds(HALF * core, HALF)],
-                    window.at[k, near_rows, :],
-                    near_send.at[k, core],
-                    near_recv.at[k, h],
-                    dev(next_chip, core),
+                    half, window.at[k, last_rows, :], last_send.at[k, core], last_recv.at[k, h], dev(prev_chip, core)
                 )
             )
-    side_weight[h] = weight_ref[...] * valid_ref[...].astype(F32)
-    start(remote(segment_ref, side_segment.at[h], side_send.at[0], side_recv.at[0], pair))
-    for k in range(2):
+            start(
+                remote(
+                    half, window.at[k, first_rows, :], first_send.at[k, core], first_recv.at[k, h], dev(next_chip, core)
+                )
+            )
         start(
             remote(
                 rows.at[k, :, other_cols], window.at[k, own_rows, :], own_send.at[k], own_recv.at[k], pair
             )
         )
+    for core in range(2):
+        start(
+            remote(side_mine, side_weight.at[h], side_send.at[1, core], side_recv.at[1, h], dev(prev_chip, core))
+        )
     tell(0, [along_z(1), along_z(-1)])
     tell(1, [along_y(1), along_y(-1)])
     for k in range(2):
         window[k, own_rows, :] = rows[k, :, my_cols]
-    side_segment[h] = segment_ref[...]
-    start(remote(side_weight.at[h], side_weight.at[h], side_send.at[1], side_recv.at[1], pair))
 
     flip = (
         lax.broadcasted_iota(jnp.int32, (TAPS, TAPS), 0) + lax.broadcasted_iota(jnp.int32, (TAPS, TAPS), 1)
         == TAPS - 1
     ).astype(F32).astype(BF16)
-    first_row = jnp.where(chip == 0, TAPS, jnp.where(chip == 1, TAPS // 2, 0))
+    first_row = jnp.where(chip == CHIPS - 1, TAPS, jnp.where(chip == 0, SPAN, 0))
     lane = lax.broadcasted_iota(jnp.int32, (SPAN, WINDOW), 1)
-    arrived(side_segment.at[other], side_recv.at[0])
+    for core in range(2):
+        arrived(side_segment.at[core], side_recv.at[0, core])
     segments = jnp.concatenate([side_segment[0], side_segment[1]], axis=1)
     selector = (lax.broadcasted_iota(jnp.int32, (SEGS, SPAN), 0) == segments).astype(F32).astype(BF16)
 
@@ -185,43 +224,34 @@
         skewed = pltpu.roll(wide, 1, 1, stride=1, stride_axis=0)
         toeplitz[k] = jnp.where(lane >= first_row, skewed, 0.0).astype(BF16)
 
-    def pass_on(k):
-        for core in range(2):
-            arrived(window.at[k, pl.ds(TAPS // 2 + EP * core, EP), :], near_recv.at[k, core])
-        start(
-            remote(
-                window.at[k, pl.ds(TAPS // 2, TAPS // 2), :],
-                window.at[k, pl.ds(0, TAPS // 2), :],
-                far_send.at[k],
-                far_recv.at[k],
-                dev(next_chip, h),
-            )
-        )
-
+    loads[4].wait()
+    loads[5].wait()
     build(0)
-    pass_on(0)
     pl.semaphore_wait(token.at[0], 2)
     pl.semaphore_wait(token.at[1], 2)
     tell(2, [along_z(2), along_z(-2)])
     tell(3, [along_y(2), along_y(-2)])
-    pass_on(1)
-    build(1)
-    pl.semaphore_wait(token.at[2], 2)
-    pl.semaphore_wait(token.at[3], 2)
-    tell(4, [along_z(4), along_z(-4)])
-
-    def piece(k, at, part):
-        return gathered[k].at[at, pl.ds(part * HALF // 2, HALF // 2)]
-
-    def send_piece(k, at, part, which, x_to):
-        start(remote(piece(k, at, part), piece(k, at, part), col_send.at[k, which], col_recv.at[k, which], dev(chip, h, x_to)))
+
+    def piece(k, at, side):
+        return gathered[k].at[at, pl.ds(side * HALF // 2, HALF // 2)]
+
+    def send_piece(k, at, side, which, x_to):
+        start(remote(piece(k, at, side), piece(k, at, side), col_send.at[k, which], col_recv.at[k, which], dev(chip, h, x_to)))
+
+    def part(k, at):
+        span = pl.ds(SPAN * at, SPAN)
+        return jnp.dot(toeplitz[k, :, span], window[k, span, :], preferred_element_type=F32)
 
     def filter_and_send(k):
-        arrived(window.at[k, pl.ds(pl.multiple_of(TAPS + EP * other, EP), EP), :], own_recv.at[k])
-        near = jnp.dot(toeplitz[k, :, TAPS // 2 :], window[k, TAPS // 2 :, :], preferred_element_type=F32)
-        arrived(window.at[k, pl.ds(0, TAPS // 2), :], far_recv.at[k])
-        far = jnp.dot(toeplitz[k, :, : TAPS // 2], window[k, : TAPS // 2, :], preferred_element_type=F32)
-        gathered[k][x] = (near + far).T.astype(BF16)
+        arrived(window.at[k, pl.ds(pl.multiple_of(SPAN + EP * other, EP), EP), :], own_recv.at[k])
+        added = part(k, 1)
+        for core in range(2):
+            arrived(window.at[k, pl.ds(EP * core, EP), :], first_recv.at[k, core])
+        added = added + part(k, 0)
+        for core in range(2):
+            arrived(window.at[k, pl.ds(2 * SPAN + EP * core, EP), :], last_recv.at[k, core])
+        added = added + part(k, 2)
+        gathered[k][x] = added.T.astype(BF16)
         send_piece(k, x, 0, 0, x_up)
         send_piece(k, x, 1, 1, x_down)
         send_piece(k, x, 1, 2, x_up)
@@ -267,11 +297,16 @@
                 gram_y[b] += product[:, :, HALF:]
 
     filter_and_send(0)
+    build(1)
+    pl.semaphore_wait(token.at[2], 2)
+    pl.semaphore_wait(token.at[3], 2)
+    tell(4, [along_z(4), along_z(-4)])
+    filter_and_send(1)
+    relay(0)
     pl.semaphore_wait(token.at[4], 2)
     tell(5, [pair])
-    relay(0)
-    filter_and_send(1)
-    arrived(side_weight.at[other], side_recv.at[1])
+    for core in range(2):
+        arrived(side_weight.at[core], side_recv.at[1, core])
     scale(0)
     relay(1)
     multiply(0)
@@ -312,12 +347,12 @@
         )
 
     def yf_copies():
-        out = [remote(total_y.at[z], y_final.at[0], yf_send.at[0, 0], yf_recv.at[0], pair)]
+        out = [remote(total_y.at[z, other], y_final.at[0], yf_send.at[0, 0], yf_recv.at[0], pair)]
         for step in range(1, NZ):
             for core in range(2):
                 out.append(
                     remote(
-                        total_y.at[lax.rem(z + step, NZ)],
+                        total_y.at[lax.rem(z + step, NZ), core],
                         y_final.at[step],
                         yf_send.at[step, core],
                         yf_recv.at[step],
@@ -332,24 +367,26 @@
         for step in range(1, NY):
             arrived(y_slots.at[step], y_recv.at[step])
             added = added + y_slots[step]
-        total_y[...] = added
+        total_y[:, 0] = added[:, :4]
+        total_y[:, 1] = added[:, 4:]
         copies = yf_copies()
         for step in (8, 7, 9, 6, 10, 5, 11, 4, 12, 3, 13, 2, 14, 1, 15):
             copies[2 * step - 1].start()
             copies[2 * step].start()
         copies[0].start()
-        y_final[0] = total_y[z]
+        y_final[0] = total_y[z, h]
 
     summed = collect(0, z)
     for index in range(2):
         arrived(z_tops.at[index], top_recv.at[index])
         summed = summed + z_tops[index]
-    total_z[...] = summed
+    total_z[:, 0] = summed[:, :4]
+    total_z[:, 1] = summed[:, 4:]
 
     def zf_copy(b, core):
         step = lax.rem(2 * b + h - y + NY, NY)
         return remote(
-            total_z.at[b], z_final.at[step], zf_send.at[b, core], zf_recv.at[step], dev((2 * b + h) * NZ + z, core)
+            total_z.at[b, core], z_final.at[step], zf_send.at[b, core], zf_recv.at[step], dev((2 * b + h) * NZ + z, core)
         )
 
     def for_each_zf(act):
@@ -364,7 +401,7 @@
 
     @pl.when(keeps)
     def _():
-        z_final[0] = total_z[y // 2]
+        z_final[0] = total_z[y // 2, h]
 
     @pl.when(jnp.logical_not(keeps))
     def _():
@@ -379,8 +416,7 @@
     for step in range(1, NY):
         arrived(z_final.at[step], zf_recv.at[step])
         left = left + z_final[step]
-    result = jnp.concatenate([left, right], axis=1) * (1.0 / 65536.0)
-    out_ref[...] = jnp.where(h == 0, result[:4], result[4:])
+    out_ref[...] = jnp.concatenate([left, right], axis=1) * (1.0 / 65536.0)
 
     for copy in sends:
         copy.wait_send()
@@ -405,11 +441,18 @@
     return pl.pallas_call(
         kernel,
         out_shape=jax.ShapeDtypeStruct((4, CB), F32),
-        in_specs=[vmem] * 5 + [pl.BlockSpec(memory_space=pltpu.SMEM)],
+        in_specs=[pl.BlockSpec(memory_space=pl.ANY)] * 6,
         out_specs=vmem,
         scratch_shapes=[
+            pltpu.VMEM((EP, 2, CB), BF16),
+            pltpu.VMEM((SEGS, 2, TAPS), BF16),
+            pltpu.VMEM((1, EP), jnp.int32),
+            pltpu.VMEM((1, EP), jnp.int32),
+            pltpu.VMEM((2, EP), F32),
+            pltpu.SMEM((BLOCKS,), jnp.int32),
             pltpu.VMEM((2, EP, CB), BF16),
             pltpu.VMEM((2, WINDOW, HALF), BF16),
+            pltpu.VMEM((2, EP), F32),
             pltpu.VMEM((2, 2, EP), F32),
             pltpu.VMEM((2, 1, EP), jnp.int32),
             pltpu.VMEM((2, SPAN, WINDOW), BF16),
@@ -421,19 +464,19 @@
             pltpu.VMEM((kinds, BLOCKS, 8, HALF), F32),
             pltpu.VMEM((2, BLOCKS, 8, HALF), F32),
             pltpu.VMEM((2, BLOCKS, 8, HALF), F32),
-            pltpu.VMEM((BLOCKS, 8, HALF), F32),
-            pltpu.VMEM((NY, 8, HALF), F32),
+            pltpu.VMEM((BLOCKS, 2, 4, HALF), F32),
+            pltpu.VMEM((NY, 4, HALF), F32),
             pltpu.VMEM((NY, NZ, 8, HALF), F32),
-            pltpu.VMEM((NZ, 8, HALF), F32),
-            pltpu.VMEM((NZ, 8, HALF), F32),
+            pltpu.VMEM((NZ, 2, 4, HALF), F32),
+            pltpu.VMEM((NZ, 4, HALF), F32),
+            dma((2, 2)),
+            dma((2, 2)),
             dma((2, 2)),
             dma((2, 2)),
             dma((2,)),
             dma((2,)),
-            dma((2,)),
-            dma((2,)),
-            dma((2,)),
-            dma((2,)),
+            dma((2, 2)),
+            dma((2, 2)),
             dma((2, 6)),
             dma((2, 6)),
             dma((2,)),
@@ -449,6 +492,7 @@
             dma((NZ, 2)),
             dma((NZ,)),
             pltpu.SemaphoreType.REGULAR((6,)),
+            dma((6,)),
         ],
         compiler_params=pltpu.CompilerParams(collective_id=0, has_side_effects=True),
     )(design, filter_taps, segment.reshape(1, EP), valid_flags.reshape(1, EP), weights, block_ids)

time: 61.4 us -> 57.2 us (0.932)
  Pallas kernels: 59.9 us -> 55.4 us
    pallas_call x1, Pallas kernels: 59.9 us -> 55.4 us  [body(): pl.pallas_call(kernel, out_shape=jax.ShapeDtypeStruct((4, CB), F32), in_s...]
where the time goes in v3:
time: 57.2 us; the launch traced here: 56.7 us
  Pallas kernels  55.4 us (97%)
  local copies, waits for them, and re-layouts  1.28 us (2%)
    pallas_call x1, Pallas kernels, body(): pl.pallas_call(kernel, out_shape=jax.ShapeDtypeStruct((4, CB), F32), in_s...  55.4 us
    unnamed x1, local copies, waits for them, and re-layouts  1.28 us

profile of v3, /device:TPU:1, one launch (start us, length us, event | category | flops | bytes accessed | tf_op | source)
XLA Modules:
  0.0 56.7 jit_solution(15902137673339165748)
XLA Ops:
  0.0 55.4 %shard_map.64 = f32[4,256]{1,0:T(4,128)} custom-call(bf16[128,2,256]{2,1,0:T(2,128)(2,1)} %design_in.1, bf16[256,2,512]{2,1,0:T(2,128)(2,1)} %taps_in.1, s32[1,128]{1,0:T(1,128)} %bitcast.2, s32[1,128]{1,0:T(1,128)} %bitcast.3, f32[2,128]{1,0:T(2,128)} %weight_in.1, s32[4]{0:T(128)} %ids_in.1), custom_call_target="tpu_custom_call" | custom-call | tf_op jit(solution)/shard_map/pallas_call | solution.py:441
  55.4 1.3 %copy.8 = f32[4,256]{1,0:T(4,128)} copy(f32[4,256]{1,0:T(4,128)} %shard_map.64) | data formatting | bytes 8192

commit v4 on v3

--- a/solution.py
+++ b/solution.py
@@ -278,9 +278,32 @@
         scaled[k, h] = (gathered[k][block_of(x)].astype(F32) * row_weight).astype(BF16)
         start(remote(scaled.at[k, h], scaled.at[k, h], q_send.at[k], q_recv.at[k], pair))
 
-    def y_copy(b):
-        step = lax.rem(2 * b + h - y + NY, NY)
-        return remote(gram_y.at[b], y_slots.at[step], y_send.at[b], y_recv.at[step], dev((2 * b + h) * NZ + z, h))
+    first_step = jnp.where(keeps, NY // 2, NY // 2 - 1)
+
+    def place(b):
+        return lax.rem(2 * b + h - y - first_step + 2 * NY, NY) // 2
+
+    def y_copy(at, part):
+        step = lax.rem(2 * at + first_step, NY)
+        span = pl.ds(part * NZ // 2, NZ // 2)
+        return remote(
+            gram_y.at[at, span],
+            y_slots.at[step, span],
+            y_send.at[at, part],
+            y_recv.at[step, part],
+            along_y(2 * at + first_step),
+        )
+
+    def for_each_y(part, act):
+        for at in range(BLOCKS):
+            if at == 2:
+
+                @pl.when(jnp.logical_not(keeps))
+                def _():
+                    act(y_copy(at, part))
+
+            else:
+                act(y_copy(at, part))
 
     def multiply(k):
         arrived(scaled.at[k, other], q_recv.at[k])
@@ -289,12 +312,17 @@
             product = lax.dot_general(
                 gathered[k][block_of(b)], right, (((1,), (1,)), ((), ())), preferred_element_type=F32
             ).reshape(NZ, 8, CB)
+            at = place(b)
             if k == 0:
-                gram_z[:, b] = product[:, :, :HALF]
-                gram_y[b] = product[:, :, HALF:]
+                gram_z[:, at] = product[:, :, :HALF]
             else:
-                gram_z[:, b] += product[:, :, :HALF]
-                gram_y[b] += product[:, :, HALF:]
+                gram_z[:, at] += product[:, :, :HALF]
+            for row in range(NZ):
+                turned = lax.rem(row - z - 4 + 2 * NZ, NZ)
+                if k == 0:
+                    gram_y[at, turned] = product[row, :, HALF:]
+                else:
+                    gram_y[at, turned] += product[row, :, HALF:]
 
     filter_and_send(0)
     build(1)
@@ -307,101 +335,123 @@
     tell(5, [pair])
     for core in range(2):
         arrived(side_weight.at[core], side_recv.at[1, core])
+    relay(1)
     scale(0)
-    relay(1)
+    scale(1)
     multiply(0)
-    scale(1)
     pl.semaphore_wait(token.at[5], 1)
     multiply(1)
 
-    for index, s in enumerate(SOURCES):
-        if index == 4:
-            for b in range(BLOCKS):
-
-                @pl.when(2 * b + h != y)
-                def _():
-                    y_copy(b).start()
-
-        start(
-            remote(
-                gram_z.at[lax.rem(z - s + NZ, NZ)],
-                z_slots.at[index],
-                z_send.at[index],
-                z_recv.at[index],
-                along_z(COLLECTOR[s] - s),
-            )
-        )
-
-    def collect(into, own):
-        added = gram_z[own]
+    def z_pair(part):
+        return pl.ds(2 * part, 2)
+
+    def send_z(part, near):
+        for index, s in enumerate(SOURCES):
+            if (COLLECTOR[s] == 0) == near:
+                start(
+                    remote(
+                        gram_z.at[lax.rem(z - s + NZ, NZ), z_pair(part)],
+                        z_slots.at[index, z_pair(part)],
+                        z_send.at[index, part],
+                        z_recv.at[index, part],
+                        along_z(COLLECTOR[s] - s),
+                    )
+                )
+
+    send_z(0, False)
+    for_each_y(0, lambda copy: copy.start())
+    send_z(1, False)
+    for_each_y(1, lambda copy: copy.start())
+    send_z(0, True)
+    send_z(1, True)
+
+    def collect(into, own, part):
+        added = gram_z[own, z_pair(part)]
         for index, s in enumerate(SOURCES):
             if COLLECTOR[s] == into:
-                arrived(z_slots.at[index], z_recv.at[index])
-                added = added + z_slots[index]
+                arrived(z_slots.at[index, z_pair(part)], z_recv.at[index, part])
+                added = added + z_slots[index, z_pair(part)]
         return added
 
-    for index, place in enumerate((-5, 5)):
-        middle[index] = collect(place, lax.rem(z - place + NZ, NZ))
-        start(
-            remote(middle.at[index], z_tops.at[index], top_send.at[index], top_recv.at[index], along_z(-place))
-        )
-
-    def yf_copies():
-        out = [remote(total_y.at[z, other], y_final.at[0], yf_send.at[0, 0], yf_recv.at[0], pair)]
-        for step in range(1, NZ):
+    for part in range(2):
+        for index, to in enumerate((-5, 5)):
+            middle[index, z_pair(part)] = collect(to, lax.rem(z - to + NZ, NZ), part)
+            start(
+                remote(
+                    middle.at[index, z_pair(part)],
+                    z_tops.at[index, z_pair(part)],
+                    top_send.at[index, part],
+                    top_recv.at[index, part],
+                    along_z(-to),
+                )
+            )
+
+    def yf_copies(part):
+        out = []
+        for step in ((8, 7, 9, 6, 10, 5, 11, 4), (12, 3, 13, 2, 14, 1, 15, 0))[part]:
             for core in range(2):
-                out.append(
-                    remote(
-                        total_y.at[lax.rem(z + step, NZ), core],
-                        y_final.at[step],
-                        yf_send.at[step, core],
-                        yf_recv.at[step],
-                        along_z(step, core),
+                if step:
+                    out.append(
+                        remote(
+                            total_y.at[(step - 4) % NZ, core],
+                            y_final.at[step],
+                            yf_send.at[step, core],
+                            yf_recv.at[step],
+                            along_z(step, core),
+                        )
                     )
-                )
+        if part == 1:
+            out.append(remote(total_y.at[NZ - 4, other], y_final.at[0], yf_send.at[0, 0], yf_recv.at[0], pair))
         return out
 
     @pl.when(keeps)
     def _():
-        added = gram_y[y // 2]
-        for step in range(1, NY):
-            arrived(y_slots.at[step], y_recv.at[step])
-            added = added + y_slots[step]
-        total_y[:, 0] = added[:, :4]
-        total_y[:, 1] = added[:, 4:]
-        copies = yf_copies()
-        for step in (8, 7, 9, 6, 10, 5, 11, 4, 12, 3, 13, 2, 14, 1, 15):
-            copies[2 * step - 1].start()
-            copies[2 * step].start()
-        copies[0].start()
-        y_final[0] = total_y[z, h]
-
-    summed = collect(0, z)
-    for index in range(2):
-        arrived(z_tops.at[index], top_recv.at[index])
-        summed = summed + z_tops[index]
-    total_z[:, 0] = summed[:, :4]
-    total_z[:, 1] = summed[:, 4:]
-
-    def zf_copy(b, core):
-        step = lax.rem(2 * b + h - y + NY, NY)
+        for part in range(2):
+            span = pl.ds(part * NZ // 2, NZ // 2)
+            added = gram_y[2, span]
+            for step in range(1, NY):
+                arrived(y_slots.at[step, span], y_recv.at[step, part])
+                added = added + y_slots[step, span]
+            total_y[span, 0] = added[:, :4]
+            total_y[span, 1] = added[:, 4:]
+            for copy in yf_copies(part):
+                copy.start()
+        y_final[0] = total_y[NZ - 4, h]
+
+    def zf_copy(at, core):
+        step = lax.rem(2 * at + first_step, NY)
         return remote(
-            total_z.at[b, core], z_final.at[step], zf_send.at[b, core], zf_recv.at[step], dev((2 * b + h) * NZ + z, core)
-        )
-
-    def for_each_zf(act):
-        for b in range(BLOCKS):
+            total_z.at[at, core],
+            z_final.at[step],
+            zf_send.at[at, core],
+            zf_recv.at[step],
+            along_y(2 * at + first_step, core),
+        )
+
+    def for_each_zf(part, act):
+        for at in (2 * part, 2 * part + 1):
             for core in range(2):
-
-                @pl.when(jnp.logical_not(jnp.logical_and(2 * b + h == y, h == core)))
-                def _():
-                    act(zf_copy(b, core))
-
-    for_each_zf(lambda copy: copy.start())
+                if at == 2:
+
+                    @pl.when(jnp.logical_not(jnp.logical_and(keeps, h == core)))
+                    def _():
+                        act(zf_copy(at, core))
+
+                else:
+                    act(zf_copy(at, core))
+
+    for part in range(2):
+        summed = collect(0, z, part)
+        for index in range(2):
+            arrived(z_tops.at[index, z_pair(part)], top_recv.at[index, part])
+            summed = summed + z_tops[index, z_pair(part)]
+        total_z[z_pair(part), 0] = summed[:, :4]
+        total_z[z_pair(part), 1] = summed[:, 4:]
+        for_each_zf(part, lambda copy: copy.start())
 
     @pl.when(keeps)
     def _():
-        z_final[0] = total_z[y // 2, h]
+        z_final[0] = total_z[2, h]
 
     @pl.when(jnp.logical_not(keeps))
     def _():
@@ -420,18 +470,15 @@
 
     for copy in sends:
         copy.wait_send()
-    for b in range(BLOCKS):
-
-        @pl.when(2 * b + h != y)
-        def _():
-            y_copy(b).wait_send()
-
-    for_each_zf(lambda copy: copy.wait_send())
+    for part in range(2):
+        for_each_y(part, lambda copy: copy.wait_send())
+        for_each_zf(part, lambda copy: copy.wait_send())
 
     @pl.when(keeps)
     def _():
-        for copy in yf_copies():
-            copy.wait_send()
+        for part in range(2):
+            for copy in yf_copies(part):
+                copy.wait_send()
 
 
 def body(design, filter_taps, segment, valid_flags, weights, block_ids):
@@ -481,14 +528,14 @@
             dma((2, 6)),
             dma((2,)),
             dma((2,)),
-            dma((kinds,)),
-            dma((kinds,)),
-            dma((2,)),
-            dma((2,)),
+            dma((kinds, 2)),
+            dma((kinds, 2)),
+            dma((2, 2)),
+            dma((2, 2)),
             dma((BLOCKS, 2)),
             dma((NY,)),
-            dma((BLOCKS,)),
-            dma((NY,)),
+            dma((BLOCKS, 2)),
+            dma((NY, 2)),
             dma((NZ, 2)),
             dma((NZ,)),
             pltpu.SemaphoreType.REGULAR((6,)),

time: 57.2 us -> 56.2 us (0.983)
  Pallas kernels: 55.4 us -> 54.7 us
    pallas_call x1, Pallas kernels: 55.4 us -> 54.7 us  [body(): pl.pallas_call(kernel, out_shape=jax.ShapeDtypeStruct((4, CB), F32), in_s...]
where the time goes in v4:
time: 56.2 us; the launch traced here: 56 us
  Pallas kernels  54.7 us (97%)
  local copies, waits for them, and re-layouts  1.28 us (2%)
    pallas_call x1, Pallas kernels, body(): pl.pallas_call(kernel, out_shape=jax.ShapeDtypeStruct((4, CB), F32), in_s...  54.7 us
    unnamed x1, local copies, waits for them, and re-layouts  1.28 us

profile of v4, /device:TPU:1, one launch (start us, length us, event | category | flops | bytes accessed | tf_op | source)
XLA Modules:
  0.0 56.0 jit_solution(13725667527147064141)
XLA Ops:
  0.0 54.7 %shard_map.64 = f32[4,256]{1,0:T(4,128)} custom-call(bf16[128,2,256]{2,1,0:T(2,128)(2,1)} %design_in.1, bf16[256,2,512]{2,1,0:T(2,128)(2,1)} %taps_in.1, s32[1,128]{1,0:T(1,128)} %bitcast.2, s32[1,128]{1,0:T(1,128)} %bitcast.3, f32[2,128]{1,0:T(2,128)} %weight_in.1, s32[4]{0:T(128)} %ids_in.1), custom_call_target="tpu_custom_call" | custom-call | tf_op jit(solution)/shard_map/pallas_call | solution.py:488
  54.7 1.3 %copy.8 = f32[4,256]{1,0:T(4,128)} copy(f32[4,256]{1,0:T(4,128)} %shard_map.64) | data formatting | bytes 8192

commit v5 on v4

--- a/solution.py
+++ b/solution.py
@@ -16,6 +16,7 @@
 BLOCKS = 4
 SPAN = 2 * EP
 WINDOW = TAPS + SPAN
+GRANT = 54 * 1024 * 1024 - 96 * 1024
 F32 = jnp.float32
 BF16 = jnp.bfloat16
 
@@ -158,8 +159,7 @@
     for device in greeted:
         pl.semaphore_signal(barrier, inc=1, device_id=device, device_id_type=MESH)
     loads[0].wait()
-    for k in range(2):
-        rows[k] = design_ref[:, k, :]
+    rows[0] = design_ref[:, 0, :]
     pl.semaphore_wait(barrier, len(greeted))
 
     first_rows = pl.ds(pl.multiple_of(EP * h, EP), EP)
@@ -168,16 +168,18 @@
     my_cols = pl.ds(pl.multiple_of(HALF * h, HALF), HALF)
     other_cols = pl.ds(pl.multiple_of(HALF * other, HALF), HALF)
 
-    for load in loads[1:4]:
-        load.wait()
-    side_mine[...] = weight_ref[...] * valid_ref[...].astype(F32)
-    for core in range(2):
-        start(
-            remote(
-                segment_ref, side_segment.at[h], side_send.at[0, core], side_recv.at[0, h], dev(prev_chip, core)
-            )
-        )
     for k in range(2):
+        if k == 1:
+            for load in loads[1:4]:
+                load.wait()
+            side_mine[...] = weight_ref[...] * valid_ref[...].astype(F32)
+            for core in range(2):
+                start(
+                    remote(
+                        segment_ref, side_segment.at[h], side_send.at[0, core], side_recv.at[0, h], dev(prev_chip, core)
+                    )
+                )
+            rows[1] = design_ref[:, 1, :]
         for core in range(2):
             half = rows.at[k, :, pl.ds(HALF * core, HALF)]
             start(
@@ -541,7 +543,7 @@
             pltpu.SemaphoreType.REGULAR((6,)),
             dma((6,)),
         ],
-        compiler_params=pltpu.CompilerParams(collective_id=0, has_side_effects=True),
+        compiler_params=pltpu.CompilerParams(collective_id=0, has_side_effects=True, vmem_limit_bytes=GRANT),
     )(design, filter_taps, segment.reshape(1, EP), valid_flags.reshape(1, EP), weights, block_ids)
 
 

time: 56.2 us -> 57 us (1.014)
  Pallas kernels: 54.7 us -> 55.5 us
    pallas_call x1, Pallas kernels: 54.7 us -> 55.5 us  [body(): pl.pallas_call(kernel, out_shape=jax.ShapeDtypeStruct((4, CB), F32), in_s...]
    unnamed x1 -> x9, local copies, waits for them, and re-layouts: 1.28 us -> 1.29 us
where the time goes in v5:
time: 57 us; the launch traced here: 56.8 us
  Pallas kernels  55.5 us (97%)
  local copies, waits for them, and re-layouts  1.29 us (2%)
    pallas_call x1, Pallas kernels, body(): pl.pallas_call(kernel, out_shape=jax.ShapeDtypeStruct((4, CB), F32), in_s...  55.5 us
    unnamed x9, local copies, waits for them, and re-layouts  1.29 us

profile of v5, /device:TPU:1, one launch (start us, length us, event | category | flops | bytes accessed | tf_op | source)
XLA Modules:
  0.0 56.8 jit_solution(13465899411715388477)
XLA Ops:
  0.0 0.0 copy-start.2
  0.0 0.0 copy-start.3
  0.0 0.0 copy-start
  0.0 0.0 copy-start.1
  0.0 0.6 %copy-done.2 = s32[128]{0:T(128)S(1)} copy-done((s32[128]{0:T(128)S(1)}, s32[128]{0:T(128)}, u32[]{:S(2)}) %copy-start.2) | copy-done | bytes 536
  0.7 0.0 copy-done.3
  0.7 0.0 copy-done
  0.7 0.0 copy-done.1
  0.7 55.5 %shard_map.64 = f32[4,256]{1,0:T(4,128)S(1)} custom-call(bf16[128,2,256]{2,1,0:T(2,128)(2,1)} %design_in.1, bf16[256,2,512]{2,1,0:T(2,128)(2,1)} %taps_in.1, s32[1,128]{1,0:T(1,128)S(1)} %bitcast.2, s32[1,128]{1,0:T(1,128)S(1)} %bitcast.3, f32[2,128]{1,0:T(2,128)S(1)} %copy-done, s32[4]{0:T(128)S(1)} %copy-done.3), custom_call_target="tpu_custom_call" | custom-call | tf_op jit(solution)/shard_map/pallas_call | solution.py:490
  56.2 0.6 %copy.8 = f32[4,256]{1,0:T(4,128)} copy(f32[4,256]{1,0:T(4,128)S(1)} %shard_map.64) | data formatting | bytes 8192
Async XLA Ops:
  0.0 0.7 %copy-start.2 = (s32[128]{0:T(128)S(1)}, s32[128]{0:T(128)}, u32[]{:S(2)}) copy-start(s32[128]{0:T(128)} %param.9) | copy-start | bytes 1540
  0.0 0.7 %copy-start.3 = (s32[4]{0:T(128)S(1)}, s32[4]{0:T(128)}, u32[]{:S(2)}) copy-start(s32[4]{0:T(128)} %ids_in.1) | copy-start | bytes 52
  0.0 0.7 %copy-start = (f32[2,128]{1,0:T(2,128)S(1)}, f32[2,128]{1,0:T(2,128)}, u32[]{:S(2)}) copy-start(f32[2,128]{1,0:T(2,128)} %weight_in.1) | copy-start | bytes 3076
  0.0 0.7 %copy-start.1 = (s32[128]{0:T(128)S(1)}, s32[128]{0:T(128)}, u32[]{:S(2)}) copy-start(s32[128]{0:T(128)} %param.8) | copy-start | bytes 1540

commit v6 on v4

--- a/solution.py
+++ b/solution.py
@@ -16,6 +16,7 @@
 BLOCKS = 4
 SPAN = 2 * EP
 WINDOW = TAPS + SPAN
+GRANT = 54 * 1024 * 1024 - 96 * 1024
 F32 = jnp.float32
 BF16 = jnp.bfloat16
 
@@ -158,8 +159,7 @@
     for device in greeted:
         pl.semaphore_signal(barrier, inc=1, device_id=device, device_id_type=MESH)
     loads[0].wait()
-    for k in range(2):
-        rows[k] = design_ref[:, k, :]
+    rows[0] = design_ref[:, 0, :]
     pl.semaphore_wait(barrier, len(greeted))
 
     first_rows = pl.ds(pl.multiple_of(EP * h, EP), EP)
@@ -178,6 +178,8 @@
             )
         )
     for k in range(2):
+        if k == 1:
+            rows[1] = design_ref[:, 1, :]
         for core in range(2):
             half = rows.at[k, :, pl.ds(HALF * core, HALF)]
             start(
@@ -541,7 +543,7 @@
             pltpu.SemaphoreType.REGULAR((6,)),
             dma((6,)),
         ],
-        compiler_params=pltpu.CompilerParams(collective_id=0, has_side_effects=True),
+        compiler_params=pltpu.CompilerParams(collective_id=0, has_side_effects=True, vmem_limit_bytes=GRANT),
     )(design, filter_taps, segment.reshape(1, EP), valid_flags.reshape(1, EP), weights, block_ids)
 
 

time: 56.2 us -> 55.6 us (0.989)
  Pallas kernels: 54.7 us -> 54.1 us
    pallas_call x1, Pallas kernels: 54.7 us -> 54.1 us  [body(): pl.pallas_call(kernel, out_shape=jax.ShapeDtypeStruct((4, CB), F32), in_s...]
    unnamed x1 -> x9, local copies, waits for them, and re-layouts: 1.28 us -> 1.29 us
where the time goes in v6:
time: 55.6 us; the launch traced here: 55.4 us
  Pallas kernels  54.1 us (97%)
  local copies, waits for them, and re-layouts  1.29 us (2%)
    pallas_call x1, Pallas kernels, body(): pl.pallas_call(kernel, out_shape=jax.ShapeDtypeStruct((4, CB), F32), in_s...  54.1 us
    unnamed x9, local copies, waits for them, and re-layouts  1.29 us

profile of v6, /device:TPU:1, one launch (start us, length us, event | category | flops | bytes accessed | tf_op | source)
XLA Modules:
  0.0 55.4 jit_solution(14269983965631976481)
XLA Ops:
  0.0 0.0 copy-start.2
  0.0 0.0 copy-start.3
  0.0 0.0 copy-start
  0.0 0.0 copy-start.1
  0.0 0.6 %copy-done.2 = s32[128]{0:T(128)S(1)} copy-done((s32[128]{0:T(128)S(1)}, s32[128]{0:T(128)}, u32[]{:S(2)}) %copy-start.2) | copy-done | bytes 536
  0.7 0.0 copy-done.3
  0.7 0.0 copy-done
  0.7 0.0 copy-done.1
  0.7 54.1 %shard_map.64 = f32[4,256]{1,0:T(4,128)S(1)} custom-call(bf16[128,2,256]{2,1,0:T(2,128)(2,1)} %design_in.1, bf16[256,2,512]{2,1,0:T(2,128)(2,1)} %taps_in.1, s32[1,128]{1,0:T(1,128)S(1)} %bitcast.2, s32[1,128]{1,0:T(1,128)S(1)} %bitcast.3, f32[2,128]{1,0:T(2,128)S(1)} %copy-done, s32[4]{0:T(128)S(1)} %copy-done.3), custom_call_target="tpu_custom_call" | custom-call | tf_op jit(solution)/shard_map/pallas_call | solution.py:490
  54.8 0.6 %copy.8 = f32[4,256]{1,0:T(4,128)} copy(f32[4,256]{1,0:T(4,128)S(1)} %shard_map.64) | data formatting | bytes 8192
Async XLA Ops:
  0.0 0.7 %copy-start.2 = (s32[128]{0:T(128)S(1)}, s32[128]{0:T(128)}, u32[]{:S(2)}) copy-start(s32[128]{0:T(128)} %param.9) | copy-start | bytes 1540
  0.0 0.7 %copy-start.3 = (s32[4]{0:T(128)S(1)}, s32[4]{0:T(128)}, u32[]{:S(2)}) copy-start(s32[4]{0:T(128)} %ids_in.1) | copy-start | bytes 52
  0.0 0.7 %copy-start = (f32[2,128]{1,0:T(2,128)S(1)}, f32[2,128]{1,0:T(2,128)}, u32[]{:S(2)}) copy-start(f32[2,128]{1,0:T(2,128)} %weight_in.1) | copy-start | bytes 3076
  0.0 0.7 %copy-start.1 = (s32[128]{0:T(128)S(1)}, s32[128]{0:T(128)}, u32[]{:S(2)}) copy-start(s32[128]{0:T(128)} %param.8) | copy-start | bytes 1540

commit v7 on v6

--- a/solution.py
+++ b/solution.py
@@ -43,6 +43,7 @@
     side_mine,
     side_weight,
     side_segment,
+    flipped_taps,
     toeplitz,
     gathered_0,
     gathered_1,
@@ -212,21 +213,22 @@
     ).astype(F32).astype(BF16)
     first_row = jnp.where(chip == CHIPS - 1, TAPS, jnp.where(chip == 0, SPAN, 0))
     lane = lax.broadcasted_iota(jnp.int32, (SPAN, WINDOW), 1)
+    loads[4].wait()
+    for k in range(2):
+        flipped_taps[k] = jnp.dot(taps_ref[:, k, :], flip, preferred_element_type=F32).astype(BF16)
     for core in range(2):
         arrived(side_segment.at[core], side_recv.at[0, core])
     segments = jnp.concatenate([side_segment[0], side_segment[1]], axis=1)
     selector = (lax.broadcasted_iota(jnp.int32, (SEGS, SPAN), 0) == segments).astype(F32).astype(BF16)
 
     def build(k):
-        tap_rows = lax.dot_general(
-            selector, taps_ref[:, k, :], (((0,), (0,)), ((), ())), preferred_element_type=F32
-        ).astype(BF16)
-        flipped = jnp.dot(tap_rows, flip, preferred_element_type=F32)
+        flipped = lax.dot_general(
+            selector, flipped_taps[k], (((0,), (0,)), ((), ())), preferred_element_type=F32
+        )
         wide = jnp.concatenate([flipped, jnp.zeros((SPAN, SPAN), F32)], axis=1)
         skewed = pltpu.roll(wide, 1, 1, stride=1, stride_axis=0)
         toeplitz[k] = jnp.where(lane >= first_row, skewed, 0.0).astype(BF16)
 
-    loads[4].wait()
     loads[5].wait()
     build(0)
     pl.semaphore_wait(token.at[0], 2)
@@ -504,6 +506,7 @@
             pltpu.VMEM((2, EP), F32),
             pltpu.VMEM((2, 2, EP), F32),
             pltpu.VMEM((2, 1, EP), jnp.int32),
+            pltpu.VMEM((2, SEGS, TAPS), BF16),
             pltpu.VMEM((2, SPAN, WINDOW), BF16),
             pltpu.VMEM((NX, HALF, SPAN), BF16),
             pltpu.VMEM((NX, HALF, SPAN), BF16),

time: 55.6 us -> 55 us (0.989)
  Pallas kernels: 54.1 us -> 53.5 us
    pallas_call x1, Pallas kernels: 54.1 us -> 53.5 us  [body(): pl.pallas_call(kernel, out_shape=jax.ShapeDtypeStruct((4, CB), F32), in_s...]
where the time goes in v7:
time: 55 us; the launch traced here: 54.9 us
  Pallas kernels  53.5 us (97%)
  local copies, waits for them, and re-layouts  1.29 us (2%)
    pallas_call x1, Pallas kernels, body(): pl.pallas_call(kernel, out_shape=jax.ShapeDtypeStruct((4, CB), F32), in_s...  53.5 us
    unnamed x9, local copies, waits for them, and re-layouts  1.29 us

profile of v7, /device:TPU:1, one launch (start us, length us, event | category | flops | bytes accessed | tf_op | source)
XLA Modules:
  0.0 54.9 jit_solution(2472772906860412233)
XLA Ops:
  0.0 0.0 copy-start.2
  0.0 0.0 copy-start.3
  0.0 0.0 copy-start
  0.0 0.0 copy-start.1
  0.0 0.6 %copy-done.2 = s32[128]{0:T(128)S(1)} copy-done((s32[128]{0:T(128)S(1)}, s32[128]{0:T(128)}, u32[]{:S(2)}) %copy-start.2) | copy-done | bytes 536
  0.7 0.0 copy-done.3
  0.7 0.0 copy-done
  0.7 0.0 copy-done.1
  0.7 53.5 %shard_map.64 = f32[4,256]{1,0:T(4,128)S(1)} custom-call(bf16[128,2,256]{2,1,0:T(2,128)(2,1)} %design_in.1, bf16[256,2,512]{2,1,0:T(2,128)(2,1)} %taps_in.1, s32[1,128]{1,0:T(1,128)S(1)} %bitcast.2, s32[1,128]{1,0:T(1,128)S(1)} %bitcast.3, f32[2,128]{1,0:T(2,128)S(1)} %copy-done, s32[4]{0:T(128)S(1)} %copy-done.3), custom_call_target="tpu_custom_call" | custom-call | tf_op jit(solution)/shard_map/pallas_call | solution.py:492
  54.3 0.6 %copy.8 = f32[4,256]{1,0:T(4,128)} copy(f32[4,256]{1,0:T(4,128)S(1)} %shard_map.64) | data formatting | bytes 8192
Async XLA Ops:
  0.0 0.7 %copy-start.2 = (s32[128]{0:T(128)S(1)}, s32[128]{0:T(128)}, u32[]{:S(2)}) copy-start(s32[128]{0:T(128)} %param.9) | copy-start | bytes 1540
  0.0 0.7 %copy-start.3 = (s32[4]{0:T(128)S(1)}, s32[4]{0:T(128)}, u32[]{:S(2)}) copy-start(s32[4]{0:T(128)} %ids_in.1) | copy-start | bytes 52
  0.0 0.7 %copy-start = (f32[2,128]{1,0:T(2,128)S(1)}, f32[2,128]{1,0:T(2,128)}, u32[]{:S(2)}) copy-start(f32[2,128]{1,0:T(2,128)} %weight_in.1) | copy-start | bytes 3076
  0.0 0.7 %copy-start.1 = (s32[128]{0:T(128)S(1)}, s32[128]{0:T(128)}, u32[]{:S(2)}) copy-start(s32[128]{0:T(128)} %param.8) | copy-start | bytes 1540
